TPU v7x, 32 devices: a whole 2x2x4 slice. The times are simulated.
32 devices in a mesh: section: 4 (over y, x), dev: 8 (over z, core).
Axes of the slice: x: 2, y: 2, z: 4, core: 2. Of those that a mesh axis runs over, the one named last changes fastest.
Arguments:
- hidden: bfloat16 [256, 2048], P('dev'), may hold values from -8 to 8
- lengths: int32 [256], P('dev'), may hold values from 1 to 256, as said below
- attn_gain: float32 [2048], replicated, may hold values from 0.1 to 1.9
- w_query: bfloat16 [2048, 3072], P(None, 'section'), may hold values from -0.125 to 0.125
- w_latent: bfloat16 [2048, 512], replicated, may hold values from -0.125 to 0.125
- latent_gain: float32 [512], replicated, may hold values from 0.1 to 1.9
- w_rope_key: bfloat16 [64, 2048], replicated, may hold values from -0.125 to 0.125
- w_key_up: bfloat16 [16, 512, 128], P('section'), may hold values from -0.5 to 0.5
- w_value_up: bfloat16 [16, 512, 128], P('section'), may hold values from -0.25 to 0.25
- w_out: bfloat16 [2048, 2048], P('section'), may hold values from -0.125 to 0.125
- latent_cache: bfloat16 [256, 256, 512], P('dev'), may hold values from -6 to 6
- rope_cache: bfloat16 [256, 64, 256], P('dev'), may hold values from -1200 to 1200
- ffn_gain: float32 [2048], replicated, may hold values from 0.1 to 1.9
- expert_ids: int32 [256, 6], P('dev'), may hold values from 0 to 63, all different within a row; in each aligned block of 8 rows (0 to 7, 8 to 15, ...) at most 2 rows name the same one
- route_weights: float32 [256, 6], P('dev'), may hold values from 0.05 to 0.5
- w_gate_up: bfloat16 [64, 2, 1408, 2048], P('dev', None, 'section'), may hold values from -0.125 to 0.125
- w_down: bfloat16 [64, 1408, 2048], P('dev', 'section'), may hold values from -0.15625 to 0.15625
Outputs:
- layer_out: bfloat16 [256, 2048], P('dev')
Inputs may be any that keep to these rules, and one draw needn't show every extreme that they name: `lengths`: every aligned block of 32 rows holds a row of length 256. `expert_ids`: each row names 6 different experts. In every aligned block of 8 rows no expert is named by more than 2 rows, and some block has an expert named by exactly 2.
All inputs are finite; a program needn't handle non-finite values.
Results may differ from a plain program's by a relative error of at most 0.011.
Values may be sent and summed in bfloat16 or wider, within the bound.
A program may use at most 128 MiB of HBM per device.

v0:
```python
import jax
import jax.numpy as jnp
from jax import lax
from jax.sharding import PartitionSpec as P

EXPERTS = 64
MOST = 2


epsilon = 1e-06
far_below = -1e30


def rms_norm(values, norm_gain):
    mean_square = jnp.mean(values * values, axis=-1, keepdims=True)
    return values * lax.rsqrt(mean_square + epsilon) * norm_gain


def rotary(values, positions):
    half_width = values.shape[-1] // 2
    step_index = jnp.arange(half_width, dtype=jnp.float32)
    frequency = jnp.exp(-jnp.log(10000.0) * step_index / half_width)
    angles = positions.astype(jnp.float32)[:, None] * frequency[None, :]
    if values.ndim == 3:
        angles = angles[:, None, :]
    cosine = jnp.cos(angles)
    sine_part = jnp.sin(angles)
    first_half = values[..., :half_width]
    second = values[..., half_width:]
    return jnp.concatenate(
        [first_half * cosine - second * sine_part, second * cosine + first_half * sine_part],
        axis=-1,
    )


def slot_targets(expert_ids, block_rows):
    row_count, top_count = expert_ids.shape
    blocks = row_count // block_rows
    flat_ids = expert_ids.reshape(blocks, block_rows * top_count)
    onehot = (flat_ids[:, :, None] == jnp.arange(EXPERTS, dtype=jnp.int32)[None, None, :]).astype(
        jnp.int32
    )
    earlier = jnp.cumsum(onehot, axis=1) - onehot
    rank_in = jnp.sum(earlier * onehot, axis=2)
    capacity = blocks * MOST
    target = flat_ids * capacity + jnp.arange(blocks, dtype=jnp.int32)[:, None] * MOST + rank_in
    return (target.reshape(row_count, top_count), capacity)


def pack_rows(source, target, capacity):
    slot_count = EXPERTS * capacity
    hit_table = (
        target[:, :, None] == jnp.arange(slot_count, dtype=jnp.int32)[None, None, :]
    ).astype(jnp.bfloat16)
    hit_table = jnp.sum(hit_table, axis=1)
    packed = lax.dot_general(
        hit_table, source, (((0,), (0,)), ((), ())), preferred_element_type=jnp.float32
    )
    return packed.astype(jnp.bfloat16)


def expert_part(slot_rows, w_gate_up, w_down):
    gate_up = jnp.einsum(
        "secx,egfx->secgf", slot_rows, w_gate_up, preferred_element_type=jnp.float32
    )
    activated = (jax.nn.silu(gate_up[:, :, :, 0, :]) * gate_up[:, :, :, 1, :]).astype(jnp.bfloat16)
    return jnp.einsum("secf,efx->secx", activated, w_down, preferred_element_type=jnp.float32)


def combine_rows(middle, expert_out, target, route_weights):
    flat_out = expert_out.reshape(-1, expert_out.shape[-1])
    routed = jnp.take(flat_out, target.reshape(-1), axis=0)
    routed = routed.reshape(target.shape + (flat_out.shape[1],)).astype(jnp.float32)
    layer_out = middle.astype(jnp.float32) + jnp.sum(route_weights[:, :, None] * routed, axis=1)
    return layer_out.astype(jnp.bfloat16)


def attend(
    query_latent, query_rope, latent_new, key_new, latent_cache, rope_cache, lengths, score_scale
):
    scores = jnp.einsum(
        "rhl,rtl->rht", query_latent, latent_cache, preferred_element_type=jnp.float32
    )
    scores = scores + jnp.einsum(
        "rhp,rpt->rht", query_rope, rope_cache, preferred_element_type=jnp.float32
    )
    scores = scores * score_scale
    self_score = jnp.einsum(
        "rhl,rl->rh", query_latent, latent_new, preferred_element_type=jnp.float32
    )
    self_score = (
        self_score
        + jnp.einsum("rhp,rp->rh", query_rope, key_new, preferred_element_type=jnp.float32)
    ) * score_scale
    places = jnp.arange(latent_cache.shape[1], dtype=jnp.int32)
    valid_mask = places[None, None, :] < lengths[:, None, None]
    masked = jnp.where(valid_mask, scores, far_below)
    peak_score = jnp.maximum(jnp.max(masked, axis=2), self_score)
    weights = jnp.where(valid_mask, jnp.exp(masked - peak_score[:, :, None]), 0.0)
    self_weight = jnp.exp(self_score - peak_score)
    totals = jnp.sum(weights, axis=2) + self_weight
    prob_cache = (weights / totals[:, :, None]).astype(jnp.bfloat16)
    prob_self = (self_weight / totals).astype(jnp.bfloat16)
    mixed = jnp.einsum("rht,rtl->rhl", prob_cache, latent_cache, preferred_element_type=jnp.float32)
    mixed = (
        mixed
        + prob_self.astype(jnp.float32)[:, :, None] * latent_new.astype(jnp.float32)[:, None, :]
    )
    return mixed.astype(jnp.bfloat16)


def per_device(
    hidden,
    lengths,
    attn_gain,
    w_query,
    w_latent,
    latent_gain,
    w_rope_key,
    w_key_up,
    w_value_up,
    w_out,
    latent_cache,
    rope_cache,
    ffn_gain,
    expert_ids,
    route_weights,
    w_gate_up,
    w_down,
):
    sections = lax.axis_size("section")
    devices = lax.axis_size("dev")
    row_count = hidden.shape[0]
    quarter = row_count // sections
    model_width = hidden.shape[1]
    head_local = w_key_up.shape[0]
    nope_width = w_key_up.shape[2]
    rope_width = w_rope_key.shape[0]
    score_scale = (nope_width + rope_width) ** (-0.5)
    normed = rms_norm(hidden.astype(jnp.float32), attn_gain).astype(jnp.bfloat16)
    queries = jnp.dot(normed, w_query, preferred_element_type=jnp.float32).astype(jnp.bfloat16)
    queries = queries.reshape(row_count, head_local, nope_width + rope_width)
    query_rope = rotary(queries[:, :, nope_width:].astype(jnp.float32), lengths).astype(
        jnp.bfloat16
    )
    query_latent = jnp.einsum(
        "rhn,hln->rhl", queries[:, :, :nope_width], w_key_up, preferred_element_type=jnp.float32
    ).astype(jnp.bfloat16)
    latent_new = rms_norm(
        jnp.dot(normed, w_latent, preferred_element_type=jnp.float32), latent_gain
    ).astype(jnp.bfloat16)
    key_raw = lax.dot_general(
        normed, w_rope_key, (((1,), (1,)), ((), ())), preferred_element_type=jnp.float32
    )
    key_new = rotary(key_raw, lengths).astype(jnp.bfloat16)
    mixed_latent = attend(
        query_latent,
        query_rope,
        latent_new,
        key_new,
        latent_cache,
        rope_cache,
        lengths,
        score_scale,
    )
    head_out = jnp.einsum(
        "rhl,hlv->rhv", mixed_latent, w_value_up, preferred_element_type=jnp.float32
    ).astype(jnp.bfloat16)
    heads_flat = head_out.reshape(row_count, -1)
    section_index = lax.axis_index("section")
    attention = lax.psum_scatter(
        jnp.dot(heads_flat, w_out, preferred_element_type=jnp.float32),
        "section",
        scatter_dimension=0,
        tiled=True,
    )
    first_row = section_index * quarter
    own_hidden = lax.dynamic_slice_in_dim(hidden, first_row, quarter, 0)
    own_ids = lax.dynamic_slice_in_dim(expert_ids, first_row, quarter, 0)
    own_weights = lax.dynamic_slice_in_dim(route_weights, first_row, quarter, 0)
    middle = (own_hidden.astype(jnp.float32) + attention).astype(jnp.bfloat16)
    expert_in = rms_norm(middle.astype(jnp.float32), ffn_gain).astype(jnp.bfloat16)
    target, capacity = slot_targets(own_ids, quarter)
    packed = pack_rows(expert_in, target, capacity).reshape(devices, -1, capacity, model_width)
    received = lax.all_to_all(packed, "dev", split_axis=0, concat_axis=0, tiled=True)
    partial_out = expert_part(
        lax.all_gather(received, "section", axis=2, tiled=True), w_gate_up, w_down
    )
    summed = lax.psum_scatter(
        partial_out.astype(jnp.bfloat16), "section", scatter_dimension=2, tiled=True
    )
    arrived = lax.all_to_all(summed, "dev", split_axis=0, concat_axis=0, tiled=True)
    own_out = combine_rows(middle, arrived, target, own_weights)
    return lax.all_gather(own_out, "section", axis=0, tiled=True)


def solution(mesh):
    in_specs = (
        P("dev", None),
        P("dev"),
        P(),
        P(None, "section"),
        P(),
        P(),
        P(),
        P("section", None, None),
        P("section", None, None),
        P("section", None),
        P("dev", None, None),
        P("dev", None, None),
        P(),
        P("dev", None),
        P("dev", None),
        P("dev", None, "section", None),
        P("dev", "section", None),
    )
    out_specs = P("dev", None)
    return jax.shard_map(
        per_device, mesh=mesh, in_specs=in_specs, out_specs=out_specs, check_vma=False
    )
```

profile of v0, /device:TPU:0, one launch (start us, length us, event | category | flops | bytes accessed | tf_op | source)
XLA Modules:
  0.0 231.8 jit_solution(4107624617080783444)
XLA Ops:
  6.5 0.0 all-reduce.3.cloned.1.call-start
  6.6 0.5 multiply_exponential_fusion
  7.1 1.3 fusion.25
  8.5 0.0 copy-done
  8.5 2.2 convolution_convert_fusion.2
  10.7 1.0 reshape.269
  11.8 0.1 iota_compare_fusion
  11.9 0.0 slice-start
  11.9 0.3 fusion.65
  12.1 0.9 subtract_convert_fusion.1
  13.1 0.1 maximum_bitcast_fusion
  13.1 0.1 subtract_convert_fusion
  13.3 0.2 fusion.52
  13.5 1.5 fusion.62
  15.0 2.2 multiply_reduce_fusion.1
  17.3 0.3 fusion.17
  17.5 0.0 copy-done.11
  17.6 0.1 fusion.64
  17.6 0.2 fusion.29
  17.9 5.9 %fusion.72 = (f32[32,4]{1,0:T(8,128)S(1)}, f32[32,4,256]{2,1,0:T(4,128)S(1)}) fusion(f32[32,4,256]{2,1,0:T(4,128)S(1)} %fusion.62, bf16[32,256,512]{2,1,0:T(8,128)(2,1)} %param.27, bf16[32,4,512]{2,0,1:T(8,128)(2,1)S(1)} %fusion.17, pred[32,256]{1,0:T(8,128)(4,1)S(1)} %iota_compare_fusion), kind=kOutput, calls=%fused_computation.105 | convolution fusion | flops 33685376 | bytes 8790528 | tf_op jit(solution)/shard_map/rhl,rtl->rht/dot_general | solution.py:81
  23.8 0.2 fusion.32
  24.1 1.3 fusion.16
  25.3 0.0 copy-start.13
  25.4 0.2 fusion.20
  25.6 0.3 copy-done.3
  25.8 1.2 fusion.44
  27.0 0.0 all-reduce.3.cloned.1.call-update
  27.0 0.0 all-gather.2.cloned.1.call-start
  27.1 0.1 constant_dynamic-slice_fusion
  27.2 0.1 copy.67
  27.3 0.1 eq.40
  27.3 0.1 fusion.50
  27.4 0.1 reduce_window_sum.11
  27.5 0.2 select_reduce_fusion
  27.7 0.1 reduce_sum.74
  27.8 0.1 copy.51
  27.9 0.6 dynamic-slice
  29.1 0.1 fusion.54
  29.2 43.8 %all-reduce.3.cloned.1.call-done = f32[32,2048]{1,0:T(8,128)} async-done(((f32[32,2048]{1,0:T(8,128)}), f32[32,2048]{1,0:T(8,128)}) %all-reduce.3.cloned.1.call-update) | async-done | bytes 262160
  73.0 1.0 fusion.33
  74.0 0.4 convolution_convert_fusion
  74.3 0.3 reshape.271
  74.7 19.7 %all_to_all.10 = bf16[8,8,2,2048]{3,2,1,0:T(2,128)(2,1)S(1)} all-to-all(bf16[8,8,2,2048]{3,2,1,0:T(2,128)(2,1)S(1)} %reshape.271), channel_id=1, replica_groups=mesh['section'=4,'dev'=8] {'dev'}, dimensions={0} | all-to-all | bytes 1048576 | tf_op jit(solution)/shard_map/all_to_all | solution.py:185
  94.4 1.0 copy.52
  95.4 0.0 all-gather.2.cloned.1.call-update
  95.4 0.2 reduce-scatter.2.cloned.1.call-start
  95.6 33.1 %all-gather.2.cloned.1.call-done = bf16[8,8,8,2048]{3,1,0,2:T(8,128)(2,1)} async-done(((bf16[8,8,2,2048]{3,1,0,2:T(8,128)(2,1)}), bf16[8,8,8,2048]{3,1,0,2:T(8,128)(2,1)}) %all-gather.2.cloned.1.call-update) | async-done | bytes 2097168 | tf_op jit(solution)/shard_map/all_gather | solution.py:187
  128.7 14.2 %fusion.11 = f32[8,8,8,2,352]{4,2,3,0,1:T(8,128)} fusion(bf16[8,2,352,2048]{3,2,1,0:T(8,128)(2,1)} %param.32, bf16[8,8,8,2048,1]{3,1,0,2,4:T(8,128)(2,1)} %bitcast.70), kind=kOutput, calls=%fused_computation.9 | convolution fusion | flops 1476395008 | bytes 26607616 | tf_op jit(solution)/shard_map/secx,egfx->secgf/dot_general | solution.py:63
  142.8 6.9 %fusion.7 = bf16[8,8,8,2048]{3,2,0,1:T(8,128)(2,1)S(1)} fusion(bf16[8,352,2048]{2,1,0:T(8,128)(2,1)} %param.33, f32[8,8,8,2,352]{4,2,3,0,1:T(8,128)} %fusion.11), kind=kOutput, calls=%fused_computation.6 | convolution fusion | flops 740327424 | bytes 15073280 | tf_op jit(solution)/shard_map/secf,efx->secx/dot_general | solution.py:67
  149.7 2.5 %copy.55 = bf16[8,8,8,2048]{3,1,0,2:T(8,128)(2,1)} copy(bf16[8,8,8,2048]{3,2,0,1:T(8,128)(2,1)S(1)} %fusion.7) | data formatting | bytes 4194304 | tf_op jit(solution)/shard_map/convert_element_type | solution.py:190
  152.2 0.0 reduce-scatter.2.cloned.1.call-update
  152.2 35.3 %reduce-scatter.2.cloned.1.call-done = bf16[8,8,2,2048]{3,1,0,2:T(8,128)(2,1)} async-done(((bf16[8,8,8,2048]{3,1,0,2:T(8,128)(2,1)}), bf16[8,8,2,2048]{3,1,0,2:T(8,128)(2,1)}) %reduce-scatter.2.cloned.1.call-update) | async-done | bytes 524304 | tf_op jit(solution)/shard_map/reduce_scatter | solution.py:189
  187.6 2.4 %copy.56 = bf16[8,8,2,2048]{3,2,1,0:T(2,128)(2,1)} copy(bf16[8,8,2,2048]{3,1,0,2:T(8,128)(2,1)} %reduce-scatter.2.cloned.1.call-done) | data formatting | bytes 1048576 | tf_op jit(solution)/shard_map/reduce_scatter | solution.py:189
  189.9 4.6 %all-to-all-start.1 = ((bf16[8,8,2,2048]{3,2,1,0:T(2,128)(2,1)}), bf16[8,8,2,2048]{3,2,1,0:T(2,128)(2,1)}, u32[]{:S(2)}, u32[]{:S(2)}) async-start(bf16[8,8,2,2048]{3,2,1,0:T(2,128)(2,1)} %copy.56), calls=%async_computation.2 | async-start | bytes 1048576 | tf_op jit(solution)/shard_map/all_to_all | solution.py:192
  194.6 0.1 mul.239
  194.6 0.1 constant_dynamic-slice_fusion.1
  194.7 0.1 copy.49
  194.8 15.2 %all-to-all-done.1 = bf16[8,8,2,2048]{3,2,1,0:T(2,128)(2,1)} async-done(((bf16[8,8,2,2048]{3,2,1,0:T(2,128)(2,1)}), bf16[8,8,2,2048]{3,2,1,0:T(2,128)(2,1)}, u32[]{:S(2)}, u32[]{:S(2)}) %all-to-all-start.1) | async-done | bytes 524320 | tf_op jit(solution)/shard_map/all_to_all | solution.py:192
  210.0 2.0 reshape.272
  212.0 2.7 %gather_fusion = bf16[48,2048]{1,0:T(8,128)(2,1)} fusion(bf16[128,2048]{1,0:T(8,128)(2,1)} %reshape.272, s32[1024]{0:T(1024)S(1)} %pad_clamp_fusion), kind=kCustom, calls=%fused_computation | custom fusion | bytes 393408 | tf_op jit(solution)/shard_map/jit(_take)/gather | solution.py:72
  214.7 1.0 gather.7
  215.7 0.3 multiply_reduce_fusion
  216.0 8.6 %all_gather.7 = bf16[32,2048]{1,0:T(8,128)(2,1)S(1)} all-gather(bf16[8,2048]{1,0:T(8,128)(2,1)S(1)} %fusion.36), channel_id=1, replica_groups=mesh['section'=4,'dev'=8] {'section'}, dimensions={0}, use_global_device_ids=true | all-gather | bytes 163840 | tf_op jit(solution)/shard_map/all_gather | solution.py:194
  224.6 0.7 copy.94
  (41 shorter events, 0.2 us)
Async XLA Ops:
  6.5 2.0 copy-start
  6.5 5.3 %copy-start.2 = (bf16[32,2048]{1,0:T(8,128)(2,1)S(1)}, bf16[32,2048]{1,0:T(8,128)(2,1)}, u32[]{:S(2)}) copy-start(bf16[32,2048]{1,0:T(8,128)(2,1)} %param.17) | copy-start | bytes 393220
  6.5 5.3 %copy-start.7 = (f32[2048]{0:T(1024)S(1)}, f32[2048]{0:T(1024)}, u32[]{:S(2)}) copy-start(f32[2048]{0:T(1024)} %param.19) | copy-start | bytes 24580
  6.5 5.2 %copy-start.12 = (s32[32]{0:T(128)S(1)}, s32[32]{0:T(128)}, u32[]{:S(2)}) copy-start(s32[32]{0:T(128)} %param.18) | copy-start | bytes 388
  6.5 5.3 %copy-start.6 = (bf16[64,2048]{1,0:T(8,128)(2,1)S(1)}, bf16[64,2048]{1,0:T(8,128)(2,1)}, u32[]{:S(2)}) copy-start(bf16[64,2048]{1,0:T(8,128)(2,1)} %param.23) | copy-start | bytes 786436
  6.5 66.4 %all-reduce.3.cloned.1.call-start = ((), (), s32[]{:S(2)}) async-start(), calls=%async_computation.5 | async-start | bytes 524288
  10.7 6.5 %copy-start.4 = (bf16[4,512,128]{2,1,0:T(8,128)(2,1)S(1)}, bf16[4,512,128]{2,1,0:T(8,128)(2,1)}, u32[]{:S(2)}) copy-start(bf16[4,512,128]{2,1,0:T(8,128)(2,1)} %param.24) | copy-start | bytes 1572868
  10.7 6.8 %copy-start.11 = (f32[512]{0:T(512)S(1)}, f32[512]{0:T(512)}, u32[]{:S(2)}) copy-start(f32[512]{0:T(512)} %param.22) | copy-start | bytes 6148
  11.9 12.2 %slice-start = ((s8[8388608]{0:T(1024)(128)(4,1)}), s8[4194304]{0:T(1024)(128)(4,1)S(1)}, s32[]{:S(2)}) async-start(s8[8388608]{0:T(1024)(128)(4,1)} %bitcast.68), calls=%async_computation.6 | async-start | bytes 8388608
  17.9 6.2 %slice-start.1 = ((s8[8388608]{0:T(1024)(128)(4,1)}), s8[4194304]{0:T(1024)(128)(4,1)S(1)}, s32[]{:S(2)}) async-start(s8[8388608]{0:T(1024)(128)(4,1)} %bitcast.68), calls=%async_computation.7 | async-start | bytes 8388608
  24.1 1.3 copy-start.5
  24.1 1.8 copy-start.3
  25.3 1.8 copy-start.9
  25.3 2.5 %copy-start.13 = (u32[32]{0:T(128)S(1)}, u32[32]{0:T(128)}, u32[]{:S(2)}) copy-start(u32[32]{0:T(128)} %constant.64) | copy-start | bytes 388
  25.4 48.6 %copy-start.8 = (f32[2048]{0:T(1024)S(1)}, f32[2048]{0:T(1024)}, u32[]{:S(2)}) copy-start(f32[2048]{0:T(1024)} %param.29) | copy-start | bytes 24580
  27.0 101.7 %all-gather.2.cloned.1.call-start = ((), (), s32[]{:S(2)}) async-start(), calls=%async_computation.3 | async-start | bytes 2621440 | tf_op jit(solution)/shard_map/all_gather | solution.py:187
  95.4 92.2 %reduce-scatter.2.cloned.1.call-start = ((), (), s32[]{:S(2)}) async-start(), calls=%async_computation.4 | async-start | bytes 2621440 | tf_op jit(solution)/shard_map/reduce_scatter | solution.py:189
  152.2 42.4 %copy-start.10 = (f32[32,6]{0,1:T(8,128)S(1)}, f32[32,6]{0,1:T(8,128)}, u32[]{:S(2)}) copy-start(f32[32,6]{0,1:T(8,128)} %param.31) | copy-start | bytes 2308
  152.2 73.0 %copy-start.1 = (bf16[2048,768]{1,0:T(8,128)(2,1)S(1)}, bf16[2048,768]{1,0:T(8,128)(2,1)}, u32[]{:S(2)}) copy-start(bf16[2048,768]{1,0:T(8,128)(2,1)} %param.20) | copy-start | bytes 9437188
  189.9 20.0 %all-to-all-start.1 = ((bf16[8,8,2,2048]{3,2,1,0:T(2,128)(2,1)}), bf16[8,8,2,2048]{3,2,1,0:T(2,128)(2,1)}, u32[]{:S(2)}, u32[]{:S(2)}) async-start(bf16[8,8,2,2048]{3,2,1,0:T(2,128)(2,1)} %copy.56), calls=%async_computation.2 | async-start | bytes 1048576 | tf_op jit(solution)/shard_map/all_to_all | solution.py:192
Sparse Core Ops, SparseCore 0:
  27.1 45.7 all-reduce.2
  95.5 33.1 all-gather.1
  152.3 35.1 reduce-scatter.1
where the time goes:
time: 232 us
  waiting for transfers between devices  127 us (55%)
  matrix products  36.9 us (16%)
  blocking collectives  28.3 us (12%)
  local copies, waits for them, and re-layouts  15.1 us (7%)
  between operations  14.1 us (6%)
  other arithmetic  5.1 us (2%)
  starting transfers between devices  4.92 us (2%)
    unnamed x4, waiting for transfers between devices  43.9 us
    reduce_scatter x1, waiting for transfers between devices, per_device(): lax.psum_scatter(partial_out.astype(jnp.bfloat16), 'section', scatter_dim...  35.3 us
    all_gather x1, waiting for transfers between devices, per_device(): lax.all_gather(received, 'section', axis=2, tiled=True)  33.1 us
    all_to_all x1, blocking collectives, per_device(): lax.all_to_all(packed, 'dev', split_axis=0, concat_axis=0, tiled=True)  19.7 us
    all_to_all x1, waiting for transfers between devices, per_device(): lax.all_to_all(summed, 'dev', split_axis=0, concat_axis=0, tiled=True)  15.2 us
    dot_general x1, matrix products, expert_part(): jnp.einsum('secx,egfx->secgf', slot_rows, w_gate_up, preferred_element_ty...  14.2 us
    all_gather x1, blocking collectives, per_device(): return lax.all_gather(own_out, 'section', axis=0, tiled=True)  8.58 us
    dot_general x1, matrix products, expert_part(): jnp.einsum('secf,efx->secx', activated, w_down, preferred_element_type=jn...  6.87 us
  transfers between devices with their start and end apart: 4, of which 4 were waited for; matrix products, arithmetic and copies ran while one was open for 1% of the time, Pallas kernels for 0%

commit v1 on v0

--- a/solution.py
+++ b/solution.py
@@ -1,10 +1,14 @@
+import functools
+
 import jax
 import jax.numpy as jnp
 from jax import lax
+from jax.experimental import pallas as pl
+from jax.experimental.pallas import tpu as pltpu
 from jax.sharding import PartitionSpec as P
 
-EXPERTS = 64
 MOST = 2
+MESH = pl.DeviceIdType.MESH
 
 
 epsilon = 1e-06
@@ -33,46 +37,283 @@
     )
 
 
-def slot_targets(expert_ids, block_rows):
-    row_count, top_count = expert_ids.shape
-    blocks = row_count // block_rows
-    flat_ids = expert_ids.reshape(blocks, block_rows * top_count)
-    onehot = (flat_ids[:, :, None] == jnp.arange(EXPERTS, dtype=jnp.int32)[None, None, :]).astype(
-        jnp.int32
-    )
-    earlier = jnp.cumsum(onehot, axis=1) - onehot
-    rank_in = jnp.sum(earlier * onehot, axis=2)
-    capacity = blocks * MOST
-    target = flat_ids * capacity + jnp.arange(blocks, dtype=jnp.int32)[:, None] * MOST + rank_in
-    return (target.reshape(row_count, top_count), capacity)
-
-
-def pack_rows(source, target, capacity):
-    slot_count = EXPERTS * capacity
-    hit_table = (
-        target[:, :, None] == jnp.arange(slot_count, dtype=jnp.int32)[None, None, :]
-    ).astype(jnp.bfloat16)
-    hit_table = jnp.sum(hit_table, axis=1)
-    packed = lax.dot_general(
-        hit_table, source, (((0,), (0,)), ((), ())), preferred_element_type=jnp.float32
-    )
-    return packed.astype(jnp.bfloat16)
-
-
-def expert_part(slot_rows, w_gate_up, w_down):
-    gate_up = jnp.einsum(
-        "secx,egfx->secgf", slot_rows, w_gate_up, preferred_element_type=jnp.float32
-    )
-    activated = (jax.nn.silu(gate_up[:, :, :, 0, :]) * gate_up[:, :, :, 1, :]).astype(jnp.bfloat16)
-    return jnp.einsum("secf,efx->secx", activated, w_down, preferred_element_type=jnp.float32)
-
-
-def combine_rows(middle, expert_out, target, route_weights):
-    flat_out = expert_out.reshape(-1, expert_out.shape[-1])
-    routed = jnp.take(flat_out, target.reshape(-1), axis=0)
-    routed = routed.reshape(target.shape + (flat_out.shape[1],)).astype(jnp.float32)
-    layer_out = middle.astype(jnp.float32) + jnp.sum(route_weights[:, :, None] * routed, axis=1)
-    return layer_out.astype(jnp.bfloat16)
+def route_table(own_ids, own_weights, experts, block_index):
+    hit = own_ids[:, :, None] == jnp.arange(experts, dtype=jnp.int32)[None, None, :]
+    dense = jnp.sum(jnp.where(hit, own_weights[:, :, None], 0.0), axis=1)
+    routed = jnp.any(hit, axis=1).astype(jnp.int32)
+    rank = jnp.cumsum(routed, axis=0) - routed
+    slot = jnp.where(routed > 0, block_index * MOST + rank, -1)
+    return jnp.concatenate([dense, slot.astype(jnp.float32)], axis=1)
+
+
+def expert_kernel(
+    sections,
+    devices,
+    part_ref,
+    hidden_ref,
+    gain_ref,
+    table_ref,
+    w_up_ref,
+    w_down_ref,
+    out_ref,
+    w_up,
+    w_down,
+    part_in,
+    middle,
+    row_out,
+    rows_all,
+    tables,
+    pick,
+    mix,
+    packed,
+    expert_out,
+    sum_out,
+    sum_in,
+    own_out,
+    finished,
+    up_sem,
+    down_sem,
+    part_send,
+    part_recv,
+    table_send,
+    table_recv,
+    row_send,
+    row_recv,
+    sum_send,
+    sum_recv,
+    done_send,
+    done_recv,
+):
+    section = lax.axis_index("section")
+    dev = lax.axis_index("dev")
+    total = sections * devices
+    me = dev * sections + section
+    local = w_up.shape[0]
+    rows = total * row_out.shape[0]
+    width = row_out.shape[1]
+    experts = tables.shape[2] // 2
+    slots = packed.shape[0] // local
+    f32 = jnp.float32
+
+    def up_copy(e):
+        return pltpu.make_async_copy(w_up_ref.at[e], w_up.at[e], up_sem.at[e])
+
+    def down_copy(e):
+        return pltpu.make_async_copy(w_down_ref.at[e], w_down.at[e], down_sem.at[e])
+
+    def place(t):
+        return (lax.rem(t, sections), t // sections)
+
+    def to_all(source, landing, send_sem, recv_sem):
+        def copy(i, here):
+            t = lax.rem(me + i, total)
+            return pltpu.make_async_remote_copy(
+                src_ref=source(t),
+                dst_ref=landing.at[here],
+                send_sem=send_sem.at[i],
+                recv_sem=recv_sem.at[here],
+                device_id=place(t),
+                device_id_type=MESH,
+            )
+
+        @pl.loop(1, total)
+        def _(i):
+            copy(i, me).start()
+
+        def wait_recv():
+            @pl.loop(1, total)
+            def _(i):
+                copy(i, lax.rem(me + i, total)).wait_recv()
+
+        def wait_send():
+            @pl.loop(1, total)
+            def _(i):
+                copy(i, me).wait_send()
+
+        return wait_recv, wait_send
+
+    def to_sections(source, landing, send_sem, recv_sem):
+        def copy(i, here):
+            t = lax.rem(section + i, sections)
+            return pltpu.make_async_remote_copy(
+                src_ref=source(t),
+                dst_ref=landing.at[here],
+                send_sem=send_sem.at[i],
+                recv_sem=recv_sem.at[here],
+                device_id=(t, dev),
+                device_id_type=MESH,
+            )
+
+        for i in range(1, sections):
+            copy(i, section).start()
+
+        def wait_recv():
+            for i in range(1, sections):
+                copy(i, lax.rem(section + i, sections)).wait_recv()
+
+        def wait_send():
+            for i in range(1, sections):
+                copy(i, section).wait_send()
+
+        return wait_recv, wait_send
+
+    @pl.loop(0, local)
+    def _(e):
+        up_copy(e).start()
+        down_copy(e).start()
+
+    barrier = pltpu.get_barrier_semaphore()
+
+    @pl.loop(1, total)
+    def _(i):
+        pl.semaphore_signal(
+            barrier, inc=1, device_id=place(lax.rem(me + i, total)), device_id_type=MESH
+        )
+
+    pl.semaphore_wait(barrier, total - 1)
+
+    part_recv_all, part_send_all = to_sections(
+        lambda t: part_ref.at[t], part_in, part_send, part_recv
+    )
+    table_recv_all, table_send_all = to_all(lambda t: table_ref, tables, table_send, table_recv)
+    part_in[section] = part_ref[section]
+    tables[me] = table_ref[...]
+    part_recv_all()
+    summed = part_in[0]
+    for j in range(1, sections):
+        summed = summed + part_in[j]
+    middle_rows = (hidden_ref[...].astype(f32) + summed).astype(jnp.bfloat16).astype(f32)
+    middle[...] = middle_rows
+    normed_rows = rms_norm(middle_rows, gain_ref[...]).astype(jnp.bfloat16)
+    row_out[...] = normed_rows
+    rows_all[me] = normed_rows
+    row_recv_all, row_send_all = to_all(lambda t: row_out, rows_all, row_send, row_recv)
+
+    table_recv_all()
+    table = tables[...].reshape(rows, 2 * experts)
+    lane = lax.broadcasted_iota(jnp.int32, (rows, 2 * experts), 1)
+    column = lax.broadcasted_iota(jnp.int32, (rows, local * slots), 1)
+    slot_at = jnp.full((rows, local * slots), -1.0, f32)
+    weight_at = jnp.zeros((rows, local * slots), f32)
+    for e in range(local):
+        expert = dev * local + e
+        weight_col = jnp.sum(jnp.where(lane == expert, table, 0.0), axis=1, keepdims=True)
+        slot_col = jnp.sum(jnp.where(lane == experts + expert, table, 0.0), axis=1, keepdims=True)
+        slot_col = jnp.where(slot_col < 0.0, -1.0, slot_col + float(e * slots))
+        inside = (column >= e * slots) & (column < (e + 1) * slots)
+        slot_at = jnp.where(inside, slot_col, slot_at)
+        weight_at = jnp.where(inside, weight_col, weight_at)
+    chosen = column.astype(f32) == slot_at
+    pick[...] = jnp.where(chosen, 1.0, 0.0).astype(jnp.bfloat16)
+    mix[...] = jnp.where(chosen, weight_at, 0.0).astype(jnp.bfloat16)
+
+    row_recv_all()
+    tile = 512
+
+    @pl.loop(0, width // tile)
+    def _(c):
+        span = pl.ds(pl.multiple_of(c * tile, tile), tile)
+        block = rows_all[:, :, span].astype(f32).reshape(rows, tile).astype(jnp.bfloat16)
+        packed[:, span] = lax.dot_general(
+            pick[...], block, (((0,), (0,)), ((), ())), preferred_element_type=f32
+        ).astype(jnp.bfloat16)
+
+    @pl.loop(0, local)
+    def _(e):
+        span = pl.ds(pl.multiple_of(e * slots, slots), slots)
+        up_copy(e).wait()
+        slot_rows = packed[span, :]
+        flat = (((1,), (1,)), ((), ()))
+        gate = lax.dot_general(slot_rows, w_up[e, 0], flat, preferred_element_type=f32)
+        lift = lax.dot_general(slot_rows, w_up[e, 1], flat, preferred_element_type=f32)
+        activated = (gate / (1.0 + jnp.exp(-gate)) * lift).astype(jnp.bfloat16)
+        down_copy(e).wait()
+        expert_out[span, :] = jnp.dot(
+            activated, w_down[e], preferred_element_type=f32
+        ).astype(jnp.bfloat16)
+
+    @pl.loop(0, width // tile)
+    def _(c):
+        span = pl.ds(pl.multiple_of(c * tile, tile), tile)
+        mixed = jnp.dot(mix[...], expert_out[:, span], preferred_element_type=f32)
+        sum_out[:, :, span] = mixed.reshape(total, rows // total, tile).astype(jnp.bfloat16)
+
+    sum_recv_all, sum_send_all = to_all(lambda t: sum_out.at[t], sum_in, sum_send, sum_recv)
+    sum_in[me] = sum_out[me]
+    part_send_all()
+    table_send_all()
+    row_send_all()
+    sum_recv_all()
+    result = (middle[...] + jnp.sum(sum_in[...].astype(f32), axis=0)).astype(jnp.bfloat16)
+    own_out[...] = result
+    finished[section] = result
+    done_recv_all, done_send_all = to_sections(
+        lambda t: own_out, finished, done_send, done_recv
+    )
+    sum_send_all()
+    done_recv_all()
+    out_ref[...] = finished[...]
+    done_send_all()
+
+
+def expert_layer(part, own_hidden, ffn_gain, table, w_gate_up, w_down):
+    sections = lax.axis_size("section")
+    devices = lax.axis_size("dev")
+    total = sections * devices
+    quarter, width = own_hidden.shape
+    local, _, units, _ = w_gate_up.shape
+    slots = total * MOST
+    rows = total * quarter
+    bf16, f32 = jnp.bfloat16, jnp.float32
+    vmem = pl.BlockSpec(memory_space=pltpu.VMEM)
+    anywhere = pl.BlockSpec(memory_space=pl.ANY)
+    sems = lambda count: pltpu.SemaphoreType.DMA((count,))
+    out = pl.pallas_call(
+        functools.partial(expert_kernel, sections, devices),
+        out_shape=jax.ShapeDtypeStruct((sections, quarter, width), bf16),
+        in_specs=[vmem] * 4 + [anywhere] * 2,
+        out_specs=vmem,
+        scratch_shapes=[
+            pltpu.VMEM(w_gate_up.shape, bf16),
+            pltpu.VMEM(w_down.shape, bf16),
+            pltpu.VMEM((sections, quarter, width), f32),
+            pltpu.VMEM((quarter, width), f32),
+            pltpu.VMEM((quarter, width), bf16),
+            pltpu.VMEM((total, quarter, width), bf16),
+            pltpu.VMEM((total,) + table.shape, f32),
+            pltpu.VMEM((rows, local * slots), bf16),
+            pltpu.VMEM((rows, local * slots), bf16),
+            pltpu.VMEM((local * slots, width), bf16),
+            pltpu.VMEM((local * slots, width), bf16),
+            pltpu.VMEM((total, quarter, width), bf16),
+            pltpu.VMEM((total, quarter, width), bf16),
+            pltpu.VMEM((quarter, width), bf16),
+            pltpu.VMEM((sections, quarter, width), bf16),
+            sems(local),
+            sems(local),
+            sems(sections),
+            sems(sections),
+            sems(total),
+            sems(total),
+            sems(total),
+            sems(total),
+            sems(total),
+            sems(total),
+            sems(sections),
+            sems(sections),
+        ],
+        compiler_params=pltpu.CompilerParams(
+            collective_id=0, has_side_effects=True, vmem_limit_bytes=58 * 1024 * 1024
+        ),
+    )(
+        part.reshape(sections, quarter, width),
+        own_hidden,
+        ffn_gain.reshape(1, width),
+        table,
+        w_gate_up,
+        w_down,
+    )
+    return out.reshape(sections * quarter, width)
 
 
 def attend(
@@ -132,7 +373,6 @@
     devices = lax.axis_size("dev")
     row_count = hidden.shape[0]
     quarter = row_count // sections
-    model_width = hidden.shape[1]
     head_local = w_key_up.shape[0]
     nope_width = w_key_up.shape[2]
     rope_width = w_rope_key.shape[0]
@@ -168,30 +408,14 @@
     ).astype(jnp.bfloat16)
     heads_flat = head_out.reshape(row_count, -1)
     section_index = lax.axis_index("section")
-    attention = lax.psum_scatter(
-        jnp.dot(heads_flat, w_out, preferred_element_type=jnp.float32),
-        "section",
-        scatter_dimension=0,
-        tiled=True,
-    )
     first_row = section_index * quarter
     own_hidden = lax.dynamic_slice_in_dim(hidden, first_row, quarter, 0)
     own_ids = lax.dynamic_slice_in_dim(expert_ids, first_row, quarter, 0)
     own_weights = lax.dynamic_slice_in_dim(route_weights, first_row, quarter, 0)
-    middle = (own_hidden.astype(jnp.float32) + attention).astype(jnp.bfloat16)
-    expert_in = rms_norm(middle.astype(jnp.float32), ffn_gain).astype(jnp.bfloat16)
-    target, capacity = slot_targets(own_ids, quarter)
-    packed = pack_rows(expert_in, target, capacity).reshape(devices, -1, capacity, model_width)
-    received = lax.all_to_all(packed, "dev", split_axis=0, concat_axis=0, tiled=True)
-    partial_out = expert_part(
-        lax.all_gather(received, "section", axis=2, tiled=True), w_gate_up, w_down
-    )
-    summed = lax.psum_scatter(
-        partial_out.astype(jnp.bfloat16), "section", scatter_dimension=2, tiled=True
-    )
-    arrived = lax.all_to_all(summed, "dev", split_axis=0, concat_axis=0, tiled=True)
-    own_out = combine_rows(middle, arrived, target, own_weights)
-    return lax.all_gather(own_out, "section", axis=0, tiled=True)
+    block_index = lax.axis_index("dev") * sections + section_index
+    table = route_table(own_ids, own_weights, w_gate_up.shape[0] * devices, block_index)
+    part = jnp.dot(heads_flat, w_out, preferred_element_type=jnp.float32)
+    return expert_layer(part, own_hidden, ffn_gain, table, w_gate_up, w_down)
 
 
 def solution(mesh):

time: 232 us -> 106 us (0.46)
  the two profiles are of different devices: /device:TPU:0 before, /device:TPU:25 now
where the time goes in v1:
time: 106 us
  Pallas kernels  75.7 us (71%)
  matrix products  20.8 us (20%)
  local copies, waits for them, and re-layouts  4.68 us (4%)
  other arithmetic  4.32 us (4%)
    pallas_call x1, Pallas kernels, expert_layer(): pl.pallas_call(functools.partial(expert_kernel, sections, devices), out_s...  75.7 us
    dot_general x1, matrix products, attend(): jnp.einsum('rhl,rtl->rht', query_latent, latent_cache, preferred_element_...  5.74 us
    dot_general x1, matrix products, attend(): jnp.einsum('rht,rtl->rhl', prob_cache, latent_cache, preferred_element_ty...  4.68 us
    dot_general x1, matrix products, per_device(): part = jnp.dot(heads_flat, w_out, preferred_element_type=jnp.float32)  2.74 us
    dot_general x1, matrix products, per_device(): jnp.dot(normed, w_latent, preferred_element_type=jnp.float32)  2.22 us

profile of v1, /device:TPU:25, one launch (start us, length us, event | category | flops | bytes accessed | tf_op | source)
XLA Modules:
  0.0 105.7 jit_solution(6037979886837904081)
XLA Ops:
  0.0 0.0 copy-start
  0.0 0.0 copy-start.1
  0.0 0.0 copy-start.4
  0.0 0.8 convert_element_type.60
  0.8 1.2 %fusion.7 = f32[32]{0:T(128)S(1)} fusion(bf16[32,2048]{1,0:T(8,128)(2,1)} %param.17), kind=kLoop, calls=%fused_computation.14 | loop fusion | flops 196576 | bytes 131200 | tf_op jit(solution)/shard_map/reduce_sum | solution.py:19
  2.1 0.8 constant_dynamic-slice_fusion.1
  2.8 0.1 fusion.21
  3.0 0.8 constant_dynamic-slice_fusion
  3.7 0.1 select_reduce_fusion
  3.8 0.7 pad_maximum_fusion.1.table_ref
  4.5 0.7 iota_compare_fusion
  5.2 1.3 %fusion.31 = f32[32,64]{1,0:T(8,128)S(1)} fusion(bf16[64,2048]{1,0:T(8,128)(2,1)} %param.23, bf16[32,2048]{1,0:T(8,128)(2,1)} %param.17, f32[2048]{0:T(1024)} %param.19, f32[32]{0:T(128)S(1)} %add_rsqrt_fusion.1), kind=kOutput, calls=%fused_computation.65 | convolution fusion | flops 8650752 | bytes 409728 | tf_op jit(solution)/shard_map/dot_general | solution.py:392
  6.5 0.2 subtract_convert_fusion.1
  6.7 0.1 maximum_bitcast_fusion
  6.7 1.4 %constant_dynamic-slice_fusion.2.hidden_ref = bf16[8,2048]{1,0:T(8,128)(2,1)} fusion(bf16[32,2048]{1,0:T(8,128)(2,1)} %param.17, s32[]{:T(128)S(6)} %select_n.22), kind=kLoop, calls=%fused_computation.56 | loop fusion | bytes 65540 | tf_op jit(solution)/shard_map/dynamic_slice | solution.py:412
  8.1 0.0 copy-done
  8.1 0.0 copy-start.5
  8.1 1.6 %convolution_convert_fusion.1 = bf16[32,768]{1,0:T(8,128)(2,1)S(1)} fusion(bf16[2048,768]{1,0:T(8,128)(2,1)S(1)} %copy-done, bf16[32,2048]{1,0:T(8,128)(2,1)} %param.17, f32[2048]{0:T(1024)} %param.19, f32[32]{0:T(128)S(1)} %add_rsqrt_fusion.1), kind=kOutput, calls=%fused_computation.9 | convolution fusion | flops 100950016 | bytes 3334272 | tf_op jit(solution)/shard_map/dot_general | solution.py:381
  9.7 0.1 reshape.110
  9.9 0.0 copy-start.2
  9.9 0.1 subtract_convert_fusion
  10.0 0.2 fusion.22
  10.2 1.5 %fusion.28 = f32[32,4,256]{2,1,0:T(4,128)S(1)} fusion(bf16[32,64,256]{2,1,0:T(8,128)(2,1)} %param.28, bf16[32,4,32]{2,1,0:T(4,128)(2,1)S(1)} %get-tuple-element.6, bf16[32,4,32]{2,1,0:T(4,128)(2,1)S(1)} %get-tuple-element.5), kind=kOutput, calls=%fused_computation.62 | convolution fusion | flops 4227072 | bytes 1196032 | tf_op jit(solution)/shard_map/rhp,rpt->rht/dot_general | solution.py:325
  11.8 0.0 copy-done.1
  11.8 0.0 copy-done.4
  11.8 2.2 %multiply_reduce_fusion = (f32[32]{0:T(128)S(1)}, f32[32,512]{1,0:T(8,128)S(1)}) fusion(bf16[2048,512]{1,0:T(8,128)(2,1)} %param.21, bf16[32,2048]{1,0:T(8,128)(2,1)S(1)} %copy-done.1, f32[2048]{0:T(1024)S(1)} %copy-done.4, f32[32]{0:T(128)S(1)} %add_rsqrt_fusion.1), kind=kOutput, calls=%fused_computation.28 | convolution fusion | flops 67403744 | bytes 2302208 | tf_op jit(solution)/shard_map/dot_general | solution.py:390
  14.0 0.0 copy-done.5
  14.0 0.1 fusion.30
  14.1 0.0 copy-done.2
  14.1 0.3 fusion.3
  14.4 0.3 fusion.11
  14.7 5.7 %fusion.36 = (f32[32,4]{1,0:T(8,128)S(1)}, f32[32,4,256]{2,1,0:T(4,128)S(1)}) fusion(f32[32,4,256]{2,1,0:T(4,128)S(1)} %fusion.28, bf16[32,256,512]{2,1,0:T(8,128)(2,1)} %param.27, bf16[32,4,512]{2,0,1:T(8,128)(2,1)S(1)} %fusion.3, pred[32,256]{1,0:T(8,128)(4,1)S(1)} %iota_compare_fusion), kind=kOutput, calls=%fused_computation.67 | convolution fusion | flops 33685376 | bytes 8790528 | tf_op jit(solution)/shard_map/rhl,rtl->rht/dot_general | solution.py:322
  20.4 0.2 fusion.14
  20.7 0.0 copy-start.3
  20.7 4.7 %fusion.2 = bf16[32,4,512]{2,1,0:T(4,128)(2,1)S(1)} fusion(bf16[32,256,512]{2,1,0:T(8,128)(2,1)} %param.27, f32[32,512]{1,0:T(8,128)S(1)} %get-tuple-element.8, f32[32,4]{1,0:T(8,128)S(1)} %get-tuple-element.10, f32[32,4,256]{2,1,0:T(4,128)S(1)} %get-tuple-element.18, f32[32,4]{1,0:T(8,128)S(1)} %get-tuple-element.9, f32[32,4]{1,0:T(8,128)S(1)} %fusion.25, ...), kind=kOutput, calls=%fused_computation.3 | convolution fusion | flops 33882112 | bytes 8726016 | tf_op jit(solution)/shard_map/rht,rtl->rhl/dot_general | solution.py:345
  25.3 0.0 copy-done.3
  25.3 0.2 fusion.6
  25.6 2.7 %fusion.part_ref = f32[4,8,2048]{2,1,0:T(8,128)} fusion(bf16[4,8,512]{2,1,0:T(8,128)(2,1)S(1)} %dot_general.45, bf16[512,2048]{1,0:T(8,128)(2,1)} %param.26), kind=kOutput, calls=%fused_computation | convolution fusion | flops 67108864 | bytes 2392064 | tf_op jit(solution)/shard_map/dot_general | solution.py:417
  28.4 75.7 %shard_map.163 = bf16[4,8,2048]{2,1,0:T(8,128)(2,1)} custom-call(f32[4,8,2048]{2,1,0:T(8,128)} %fusion.part_ref, bf16[8,2048]{1,0:T(8,128)(2,1)} %constant_dynamic-slice_fusion.2.hidden_ref, f32[1,2048]{1,0:T(1,128)} %bitcast.31, f32[8,128]{1,0:T(8,128)} %pad_maximum_fusion.1.table_ref, bf16[8,2,352,2048]{3,2,1,0:T(8,128)(2,1)} %w_up_ref.1, ...), custom_call_target="tpu_custom_call" | custom-call | tf_op jit(solution)/shard_map/pallas_call | solution.py:271
  104.1 1.6 %copy.53 = bf16[32,2048]{1,0:T(8,128)(2,1)} copy(bf16[32,2048]{1,0:T(8,128)(2,1)} %bitcast.26) | data formatting | bytes 262144
  (12 shorter events, 0.2 us)
Async XLA Ops:
  0.0 8.1 %copy-start = (bf16[2048,768]{1,0:T(8,128)(2,1)S(1)}, bf16[2048,768]{1,0:T(8,128)(2,1)}, u32[]{:S(2)}) copy-start(bf16[2048,768]{1,0:T(8,128)(2,1)} %param.20) | copy-start | bytes 9437188
  0.0 11.8 %copy-start.1 = (bf16[32,2048]{1,0:T(8,128)(2,1)S(1)}, bf16[32,2048]{1,0:T(8,128)(2,1)}, u32[]{:S(2)}) copy-start(bf16[32,2048]{1,0:T(8,128)(2,1)} %param.17) | copy-start | bytes 393220
  0.0 11.8 %copy-start.4 = (f32[2048]{0:T(1024)S(1)}, f32[2048]{0:T(1024)}, u32[]{:S(2)}) copy-start(f32[2048]{0:T(1024)} %param.19) | copy-start | bytes 24580
  8.1 5.9 %copy-start.5 = (f32[512]{0:T(512)S(1)}, f32[512]{0:T(512)}, u32[]{:S(2)}) copy-start(f32[512]{0:T(512)} %param.22) | copy-start | bytes 6148
  9.9 4.3 %copy-start.2 = (bf16[4,512,128]{2,1,0:T(8,128)(2,1)S(1)}, bf16[4,512,128]{2,1,0:T(8,128)(2,1)}, u32[]{:S(2)}) copy-start(bf16[4,512,128]{2,1,0:T(8,128)(2,1)} %param.24) | copy-start | bytes 1572868
  20.7 4.7 %copy-start.3 = (bf16[4,512,128]{2,1,0:T(8,128)(2,1)S(1)}, bf16[4,512,128]{2,1,0:T(8,128)(2,1)}, u32[]{:S(2)}) copy-start(bf16[4,512,128]{2,1,0:T(8,128)(2,1)} %param.25) | copy-start | bytes 1572868

commit v2 on v1

--- a/solution.py
+++ b/solution.py
@@ -69,6 +69,8 @@
     expert_out,
     sum_out,
     sum_in,
+    pair_in,
+    pair_sum,
     own_out,
     finished,
     up_sem,
@@ -81,6 +83,8 @@
     row_recv,
     sum_send,
     sum_recv,
+    pair_send,
+    pair_recv,
     done_send,
     done_recv,
 ):
@@ -238,19 +242,89 @@
         mixed = jnp.dot(mix[...], expert_out[:, span], preferred_element_type=f32)
         sum_out[:, :, span] = mixed.reshape(total, rows // total, tile).astype(jnp.bfloat16)
 
-    sum_recv_all, sum_send_all = to_all(lambda t: sum_out.at[t], sum_in, sum_send, sum_recv)
-    sum_in[me] = sum_out[me]
+    core = lax.rem(dev, 2)
+    pairs = devices // 2
+    own_pair = dev // 2
+    partner = (section, dev + 1 - 2 * core)
+
+    def pair_copy(k):
+        z = lax.rem(own_pair + 1 + k, pairs)
+        source = (2 * z + 1 - core) * sections
+        return pltpu.make_async_remote_copy(
+            src_ref=sum_out.at[pl.ds(source, sections)],
+            dst_ref=pair_in.at[z],
+            send_sem=pair_send.at[k],
+            recv_sem=pair_recv.at[k],
+            device_id=partner,
+            device_id_type=MESH,
+        )
+
+    def block_copy(z, t, here, slot):
+        return pltpu.make_async_remote_copy(
+            src_ref=pair_sum.at[z, t],
+            dst_ref=sum_in.at[here],
+            send_sem=sum_send.at[slot],
+            recv_sem=sum_recv.at[here],
+            device_id=(t, 2 * z + core),
+            device_id_type=MESH,
+        )
+
+    here = own_pair * sections + section
+
+    @pl.loop(0, pairs)
+    def _(k):
+        pair_copy(k).start()
+
+    def add_pair(k):
+        z = lax.rem(own_pair + 1 + k, pairs)
+        pair_copy(k).wait_recv()
+        mine = sum_out[pl.ds((2 * z + core) * sections, sections)].astype(f32)
+        pair_sum[z] = (mine + pair_in[z].astype(f32)).astype(jnp.bfloat16)
+        return z
+
+    @pl.loop(0, pairs - 1)
+    def _(k):
+        z = add_pair(k)
+
+        @pl.loop(0, sections)
+        def _(j):
+            t = lax.rem(section + j, sections)
+            block_copy(z, t, here, z * sections + t).start()
+
+    add_pair(pairs - 1)
+
+    @pl.loop(1, sections)
+    def _(j):
+        t = lax.rem(section + j, sections)
+        block_copy(own_pair, t, here, own_pair * sections + t).start()
+
+    sum_in[here] = pair_sum[own_pair, section]
     part_send_all()
     table_send_all()
     row_send_all()
-    sum_recv_all()
+    half = pairs * sections
+
+    @pl.loop(1, half)
+    def _(i):
+        t = lax.rem(here + i, half)
+        block_copy(t // sections, lax.rem(t, sections), t, t).wait_recv()
+
     result = (middle[...] + jnp.sum(sum_in[...].astype(f32), axis=0)).astype(jnp.bfloat16)
     own_out[...] = result
     finished[section] = result
     done_recv_all, done_send_all = to_sections(
         lambda t: own_out, finished, done_send, done_recv
     )
-    sum_send_all()
+
+    @pl.loop(1, half)
+    def _(i):
+        t = lax.rem(here + i, half)
+        block_copy(t // sections, lax.rem(t, sections), here, t).wait_send()
+
+    @pl.loop(0, pairs)
+    def _(k):
+        pair_copy(k).wait_send()
+
     done_recv_all()
     out_ref[...] = finished[...]
     done_send_all()
@@ -286,7 +360,9 @@
             pltpu.VMEM((local * slots, width), bf16),
             pltpu.VMEM((local * slots, width), bf16),
             pltpu.VMEM((total, quarter, width), bf16),
-            pltpu.VMEM((total, quarter, width), bf16),
+            pltpu.VMEM((total // 2, quarter, width), bf16),
+            pltpu.VMEM((devices // 2, sections, quarter, width), bf16),
+            pltpu.VMEM((devices // 2, sections, quarter, width), bf16),
             pltpu.VMEM((quarter, width), bf16),
             pltpu.VMEM((sections, quarter, width), bf16),
             sems(local),
@@ -297,8 +373,10 @@
             sems(total),
             sems(total),
             sems(total),
-            sems(total),
-            sems(total),
+            sems(total // 2),
+            sems(total // 2),
+            sems(devices // 2),
+            sems(devices // 2),
             sems(sections),
             sems(sections),
         ],

time: 106 us -> 97.1 us (0.916)
  the two profiles are of different devices: /device:TPU:25 before, /device:TPU:0 now
where the time goes in v2:
time: 97.1 us; the launch traced here: 96.1 us
  Pallas kernels  66.1 us (68%)
  matrix products  20.8 us (21%)
  local copies, waits for them, and re-layouts  4.68 us (5%)
  other arithmetic  4.33 us (4%)
    pallas_call x1, Pallas kernels, expert_layer(): pl.pallas_call(functools.partial(expert_kernel, sections, devices), out_s...  66.1 us
    dot_general x1, matrix products, attend(): jnp.einsum('rhl,rtl->rht', query_latent, latent_cache, preferred_element_...  5.74 us
    dot_general x1, matrix products, attend(): jnp.einsum('rht,rtl->rhl', prob_cache, latent_cache, preferred_element_ty...  4.68 us
    dot_general x1, matrix products, per_device(): part = jnp.dot(heads_flat, w_out, preferred_element_type=jnp.float32)  2.74 us
    dot_general x1, matrix products, per_device(): jnp.dot(normed, w_latent, preferred_element_type=jnp.float32)  2.22 us

profile of v2, /device:TPU:0, one launch (start us, length us, event | category | flops | bytes accessed | tf_op | source)
XLA Modules:
  0.0 96.1 jit_solution(787043451751886461)
XLA Ops:
  0.0 0.0 copy-start
  0.0 0.0 copy-start.1
  0.0 0.0 copy-start.4
  0.0 0.8 convert_element_type.60
  0.8 1.2 %fusion.7 = f32[32]{0:T(128)S(1)} fusion(bf16[32,2048]{1,0:T(8,128)(2,1)} %param.17), kind=kLoop, calls=%fused_computation.14 | loop fusion | flops 196576 | bytes 131200 | tf_op jit(solution)/shard_map/reduce_sum | solution.py:19
  2.1 0.8 constant_dynamic-slice_fusion.1
  2.8 0.1 fusion.21
  3.0 0.8 constant_dynamic-slice_fusion
  3.7 0.1 select_reduce_fusion
  3.8 0.7 pad_maximum_fusion.1.table_ref
  4.5 0.7 iota_compare_fusion
  5.2 1.3 %fusion.31 = f32[32,64]{1,0:T(8,128)S(1)} fusion(bf16[64,2048]{1,0:T(8,128)(2,1)} %param.23, bf16[32,2048]{1,0:T(8,128)(2,1)} %param.17, f32[2048]{0:T(1024)} %param.19, f32[32]{0:T(128)S(1)} %add_rsqrt_fusion.1), kind=kOutput, calls=%fused_computation.65 | convolution fusion | flops 8650752 | bytes 409728 | tf_op jit(solution)/shard_map/dot_general | solution.py:470
  6.5 0.2 subtract_convert_fusion.1
  6.7 0.1 maximum_bitcast_fusion
  6.7 1.4 %constant_dynamic-slice_fusion.2.hidden_ref = bf16[8,2048]{1,0:T(8,128)(2,1)} fusion(bf16[32,2048]{1,0:T(8,128)(2,1)} %param.17, s32[]{:T(128)S(6)} %select_n.22), kind=kLoop, calls=%fused_computation.56 | loop fusion | bytes 65540 | tf_op jit(solution)/shard_map/dynamic_slice | solution.py:490
  8.1 0.0 copy-done
  8.1 0.0 copy-start.5
  8.1 1.6 %convolution_convert_fusion.1 = bf16[32,768]{1,0:T(8,128)(2,1)S(1)} fusion(bf16[2048,768]{1,0:T(8,128)(2,1)S(1)} %copy-done, bf16[32,2048]{1,0:T(8,128)(2,1)} %param.17, f32[2048]{0:T(1024)} %param.19, f32[32]{0:T(128)S(1)} %add_rsqrt_fusion.1), kind=kOutput, calls=%fused_computation.9 | convolution fusion | flops 100950016 | bytes 3334272 | tf_op jit(solution)/shard_map/dot_general | solution.py:459
  9.7 0.1 reshape.110
  9.9 0.0 copy-start.2
  9.9 0.1 subtract_convert_fusion
  10.0 0.2 fusion.22
  10.2 1.5 %fusion.28 = f32[32,4,256]{2,1,0:T(4,128)S(1)} fusion(bf16[32,64,256]{2,1,0:T(8,128)(2,1)} %param.28, bf16[32,4,32]{2,1,0:T(4,128)(2,1)S(1)} %get-tuple-element.6, bf16[32,4,32]{2,1,0:T(4,128)(2,1)S(1)} %get-tuple-element.5), kind=kOutput, calls=%fused_computation.62 | convolution fusion | flops 4227072 | bytes 1196032 | tf_op jit(solution)/shard_map/rhp,rpt->rht/dot_general | solution.py:403
  11.8 0.0 copy-done.1
  11.8 0.0 copy-done.4
  11.8 2.2 %multiply_reduce_fusion = (f32[32]{0:T(128)S(1)}, f32[32,512]{1,0:T(8,128)S(1)}) fusion(bf16[2048,512]{1,0:T(8,128)(2,1)} %param.21, bf16[32,2048]{1,0:T(8,128)(2,1)S(1)} %copy-done.1, f32[2048]{0:T(1024)S(1)} %copy-done.4, f32[32]{0:T(128)S(1)} %add_rsqrt_fusion.1), kind=kOutput, calls=%fused_computation.28 | convolution fusion | flops 67403744 | bytes 2302208 | tf_op jit(solution)/shard_map/dot_general | solution.py:468
  14.0 0.0 copy-done.5
  14.0 0.1 fusion.30
  14.1 0.0 copy-done.2
  14.1 0.3 fusion.3
  14.4 0.3 fusion.11
  14.7 5.7 %fusion.36 = (f32[32,4]{1,0:T(8,128)S(1)}, f32[32,4,256]{2,1,0:T(4,128)S(1)}) fusion(f32[32,4,256]{2,1,0:T(4,128)S(1)} %fusion.28, bf16[32,256,512]{2,1,0:T(8,128)(2,1)} %param.27, bf16[32,4,512]{2,0,1:T(8,128)(2,1)S(1)} %fusion.3, pred[32,256]{1,0:T(8,128)(4,1)S(1)} %iota_compare_fusion), kind=kOutput, calls=%fused_computation.67 | convolution fusion | flops 33685376 | bytes 8790528 | tf_op jit(solution)/shard_map/rhl,rtl->rht/dot_general | solution.py:400
  20.4 0.2 fusion.14
  20.7 0.0 copy-start.3
  20.7 4.7 %fusion.2 = bf16[32,4,512]{2,1,0:T(4,128)(2,1)S(1)} fusion(bf16[32,256,512]{2,1,0:T(8,128)(2,1)} %param.27, f32[32,512]{1,0:T(8,128)S(1)} %get-tuple-element.8, f32[32,4]{1,0:T(8,128)S(1)} %get-tuple-element.10, f32[32,4,256]{2,1,0:T(4,128)S(1)} %get-tuple-element.18, f32[32,4]{1,0:T(8,128)S(1)} %get-tuple-element.9, f32[32,4]{1,0:T(8,128)S(1)} %fusion.25, ...), kind=kOutput, calls=%fused_computation.3 | convolution fusion | flops 33882112 | bytes 8726016 | tf_op jit(solution)/shard_map/rht,rtl->rhl/dot_general | solution.py:423
  25.3 0.0 copy-done.3
  25.3 0.2 fusion.6
  25.6 2.7 %fusion.part_ref = f32[4,8,2048]{2,1,0:T(8,128)} fusion(bf16[4,8,512]{2,1,0:T(8,128)(2,1)S(1)} %dot_general.45, bf16[512,2048]{1,0:T(8,128)(2,1)} %param.26), kind=kOutput, calls=%fused_computation | convolution fusion | flops 67108864 | bytes 2392064 | tf_op jit(solution)/shard_map/dot_general | solution.py:495
  28.4 66.1 %shard_map.163 = bf16[4,8,2048]{2,1,0:T(8,128)(2,1)} custom-call(f32[4,8,2048]{2,1,0:T(8,128)} %fusion.part_ref, bf16[8,2048]{1,0:T(8,128)(2,1)} %constant_dynamic-slice_fusion.2.hidden_ref, f32[1,2048]{1,0:T(1,128)} %bitcast.31, f32[8,128]{1,0:T(8,128)} %pad_maximum_fusion.1.table_ref, bf16[8,2,352,2048]{3,2,1,0:T(8,128)(2,1)} %w_up_ref.1, ...), custom_call_target="tpu_custom_call" | custom-call | tf_op jit(solution)/shard_map/pallas_call | solution.py:345
  94.5 1.6 %copy.53 = bf16[32,2048]{1,0:T(8,128)(2,1)} copy(bf16[32,2048]{1,0:T(8,128)(2,1)} %bitcast.26) | data formatting | bytes 262144
  (12 shorter events, 0.2 us)
Async XLA Ops:
  0.0 8.1 %copy-start = (bf16[2048,768]{1,0:T(8,128)(2,1)S(1)}, bf16[2048,768]{1,0:T(8,128)(2,1)}, u32[]{:S(2)}) copy-start(bf16[2048,768]{1,0:T(8,128)(2,1)} %param.20) | copy-start | bytes 9437188
  0.0 11.8 %copy-start.1 = (bf16[32,2048]{1,0:T(8,128)(2,1)S(1)}, bf16[32,2048]{1,0:T(8,128)(2,1)}, u32[]{:S(2)}) copy-start(bf16[32,2048]{1,0:T(8,128)(2,1)} %param.17) | copy-start | bytes 393220
  0.0 11.8 %copy-start.4 = (f32[2048]{0:T(1024)S(1)}, f32[2048]{0:T(1024)}, u32[]{:S(2)}) copy-start(f32[2048]{0:T(1024)} %param.19) | copy-start | bytes 24580
  8.1 5.9 %copy-start.5 = (f32[512]{0:T(512)S(1)}, f32[512]{0:T(512)}, u32[]{:S(2)}) copy-start(f32[512]{0:T(512)} %param.22) | copy-start | bytes 6148
  9.9 4.3 %copy-start.2 = (bf16[4,512,128]{2,1,0:T(8,128)(2,1)S(1)}, bf16[4,512,128]{2,1,0:T(8,128)(2,1)}, u32[]{:S(2)}) copy-start(bf16[4,512,128]{2,1,0:T(8,128)(2,1)} %param.24) | copy-start | bytes 1572868
  20.7 4.7 %copy-start.3 = (bf16[4,512,128]{2,1,0:T(8,128)(2,1)S(1)}, bf16[4,512,128]{2,1,0:T(8,128)(2,1)}, u32[]{:S(2)}) copy-start(bf16[4,512,128]{2,1,0:T(8,128)(2,1)} %param.25) | copy-start | bytes 1572868
